TPU v7x, 32 devices: a whole 2x2x4 slice. The times are simulated.
32 devices in a mesh: section: 4 (over z), tensor: 8 (over y, x, core).
Axes of the slice: x: 2, y: 2, z: 4, core: 2. Of those that a mesh axis runs over, the one named last changes fastest.
Arguments:
- hidden: bfloat16 [32, 8192], P('section', 'tensor'), may hold values from -33 to 33, as said below
- out_weight: bfloat16 [4096, 8192], P(('section', 'tensor')), may hold values from -12 to 12, as said below
- targets: int32 [32], replicated, may hold values from 0 to 4095
- token_mask: int32 [32], replicated, may hold values 0 or 1
Outputs:
- ce_loss: float32 [], replicated
- z_loss: float32 [], replicated
- grad_hidden: float32 [32, 8192], P('section', 'tensor')
- grad_weight: bfloat16 [4096, 8192], P(('section', 'tensor'))
Inputs may be any that keep to these rules, and one draw needn't show every extreme that they name: hidden rows of one token have one scale; entries are bounded. `out_weight`: entries are bounded.
All inputs are finite; a program needn't handle non-finite values.
Results may differ from a plain program's by a relative error of at most 0.0026.
Values may be sent and summed in bfloat16 or wider, within the bound.
No kernel may reach another device: no remote copies, remote signals or barrier semaphores. Data moves between devices by JAX's collectives and lax.ppermute only.
A program may use at most 64 MiB of HBM per device.

v0:
```python
import jax
import jax.numpy as jnp
from jax import lax
from jax.sharding import PartitionSpec as P

z_weight = 0.0001


def body(hidden, out_weight, targets, token_mask):
    vocab_dev = out_weight.shape[0]
    full_rows = lax.all_gather(hidden, "tensor", axis=1, tiled=True)
    gathered = lax.all_gather(full_rows, "section", axis=0, tiled=True)
    token_count = gathered.shape[0]
    logits = lax.dot_general(
        gathered, out_weight, (((1,), (1,)), ((), ())), preferred_element_type=jnp.float32
    )
    vocab_start = (
        lax.axis_index("section") * lax.axis_size("tensor") + lax.axis_index("tensor")
    ) * vocab_dev
    local_ids = targets - vocab_start
    target_hit = local_ids[:, None] == jnp.arange(vocab_dev, dtype=jnp.int32)[None, :]
    picked_local = jnp.sum(jnp.where(target_hit, logits, 0.0), axis=1)
    local_top = jnp.max(logits, axis=1)
    row_top = lax.pmax(local_top, ("section", "tensor"))
    local_total = jnp.sum(jnp.exp(logits - row_top[:, None]), axis=1)
    row_total, picked = lax.psum((local_total, picked_local), ("section", "tensor"))
    log_total = row_top + jnp.log(row_total)
    kept = token_mask.astype(jnp.float32)
    ce_loss = jnp.sum(kept * (log_total - picked)) / token_count
    z_loss = jnp.sum(kept * log_total * log_total) / token_count
    factor = 1.0 + 2.0 * z_weight * log_total
    probs = jnp.exp(logits - log_total[:, None])
    dlogits = (kept[:, None] * (factor[:, None] * probs - target_hit.astype(jnp.float32))).astype(
        jnp.bfloat16
    )
    grad_weight = lax.dot_general(
        dlogits, gathered, (((0,), (0,)), ((), ())), preferred_element_type=jnp.float32
    ).astype(jnp.bfloat16)
    width_part = lax.psum_scatter(
        lax.dot_general(
            out_weight, dlogits, (((0,), (1,)), ((), ())), preferred_element_type=jnp.float32
        ),
        "tensor",
        scatter_dimension=0,
        tiled=True,
    )
    mine = lax.psum_scatter(width_part, "section", scatter_dimension=1, tiled=True)
    grad_hidden = mine.T
    return (ce_loss, z_loss, grad_hidden, grad_weight)


def solution(mesh):
    placed = (P("section", "tensor"), P(("section", "tensor"), None), P(), P())
    return jax.shard_map(
        body,
        mesh=mesh,
        in_specs=placed,
        out_specs=(P(), P(), P("section", "tensor"), P(("section", "tensor"), None)),
        check_vma=False,
    )
```

profile of v0, /device:TPU:0, one launch (start us, length us, event | category | flops | bytes accessed | tf_op | source)
XLA Modules:
  0.0 185.8 jit_solution(5926214995159261907)
XLA Ops:
  7.2 0.0 copy-start
  7.2 0.0 copy-start.2
  7.2 0.0 reduce-scatter.3.cloned.1.call-start
  7.2 0.8 convert_element_type.12
  8.0 10.9 %all_gather.6 = bf16[8,8192]{1,0:T(8,128)(2,1)S(1)} all-gather(bf16[8,1024]{1,0:T(8,128)(2,1)} %param.4), channel_id=1, replica_groups=mesh['section'=4,'tensor'=8] {'tensor'}, dimensions={1}, use_global_device_ids=true | all-gather | bytes 147456 | tf_op jit(solution)/shard_map/all_gather | solution.py:11
  18.9 16.3 %all_gather.7 = bf16[32,8192]{1,0:T(8,128)(2,1)S(1)} all-gather(bf16[8,8192]{1,0:T(8,128)(2,1)S(1)} %all_gather.6), channel_id=1, replica_groups=mesh['section'=4,'tensor'=8] {'section'}, dimensions={0}, use_global_device_ids=true | all-gather | bytes 655360 | tf_op jit(solution)/shard_map/all_gather | solution.py:12
  35.2 0.0 copy-done
  35.2 0.9 fusion.1
  36.1 39.6 %pmax.7 = f32[32]{0:T(128)S(1)} all-reduce(f32[32]{0:T(128)S(1)} %get-tuple-element.12), channel_id=1, replica_groups=mesh['section'=4,'tensor'=8] {'section','tensor'}, use_global_device_ids=true, to_apply=%region_1.2 | all-reduce | flops 32 | bytes 256 | tf_op jit(solution)/shard_map/pmax | solution.py:24
  75.7 0.0 copy-done.2
  75.7 0.2 select_reduce_fusion
  75.9 41.0 %all-reduce = (f32[32]{0:T(128)S(1)}, f32[32]{0:T(128)S(1)}) all-reduce(f32[32]{0:T(128)S(1)} %get-tuple-element.5, f32[32]{0:T(128)S(1)} %get-tuple-element.4), channel_id=1, replica_groups=mesh['section'=4,'tensor'=8] {'section','tensor'}, use_global_device_ids=true, to_apply=%region_3.4 | all-reduce | flops 64 | bytes 512 | tf_op jit(solution)/shard_map/psum | solution.py:26
  116.9 0.0 copy-start.1
  116.9 1.4 convolution_bitcast_fusion
  118.3 0.0 reduce-scatter.3.cloned.1.call-update
  118.4 0.0 reduce-scatter.5.cloned.1.call-start
  118.4 0.0 copy-done.1
  118.4 0.6 fusion
  120.3 34.1 %reduce-scatter.3.cloned.1.call-done = f32[1024,32]{0,1:T(8,128)} async-done(((f32[8192,32]{0,1:T(8,128)}), f32[1024,32]{0,1:T(8,128)}) %reduce-scatter.3.cloned.1.call-update) | async-done | bytes 131088 | tf_op jit(solution)/shard_map/reduce_scatter | solution.py:39
  154.4 0.0 reduce-scatter.5.cloned.1.call-update
  154.4 2.1 %convolution_convert_fusion = bf16[128,8192]{1,0:T(8,128)(2,1)} fusion(bf16[32,8192]{1,0:T(8,128)(2,1)S(1)} %all_gather.7, f32[32,128]{1,0:T(8,128)S(1)} %get-tuple-element.13, f32[32]{0:T(128)S(1)} %get-tuple-element.11, f32[32]{0:T(128)S(1)} %get-tuple-element.10, f32[32]{0:T(128)S(1)} %convert_element_type.12, s32[32]{0:T(128)S(1)} %broadcast_subtract_fusion), kind=kOutput, calls=%fused_computation | convolution fusion | flops 68186112 | bytes 2638336 | tf_op jit(solution)/shard_map/dot_general | solution.py:36
  156.6 20.1 %reduce-scatter.5.cloned.1.call-done = f32[1024,8]{0,1:T(8,128)} async-done(((f32[1024,32]{0,1:T(8,128)}), f32[1024,8]{0,1:T(8,128)}) %reduce-scatter.5.cloned.1.call-update) | async-done | bytes 32784 | tf_op jit(solution)/shard_map/reduce_scatter | solution.py:47
  (2 shorter events, 0.0 us)
Async XLA Ops:
  7.2 28.1 %copy-start = (bf16[128,8192]{1,0:T(8,128)(2,1)S(1)}, bf16[128,8192]{1,0:T(8,128)(2,1)}, u32[]{:S(2)}) copy-start(bf16[128,8192]{1,0:T(8,128)(2,1)} %param.5) | copy-start | bytes 6291460
  7.2 68.5 %copy-start.2 = (s32[32]{0:T(128)S(1)}, s32[32]{0:T(128)}, u32[]{:S(2)}) copy-start(s32[32]{0:T(128)} %param.6) | copy-start | bytes 388
  7.2 147.2 %reduce-scatter.3.cloned.1.call-start = ((), (), s32[]{:S(2)}) async-start(), calls=%async_computation.2 | async-start | bytes 1179648 | tf_op jit(solution)/shard_map/reduce_scatter | solution.py:39
  116.9 1.5 copy-start.1
  118.4 58.3 %reduce-scatter.5.cloned.1.call-start = ((), (), s32[]{:S(2)}) async-start(), calls=%async_computation.3 | async-start | bytes 163840 | tf_op jit(solution)/shard_map/reduce_scatter | solution.py:47
Sparse Core Ops, SparseCore 0:
  118.5 35.8 reduce-scatter.2
  157.2 19.4 reduce-scatter.4
where the time goes:
time: 186 us
  blocking collectives  108 us (58%)
  waiting for transfers between devices  54.2 us (29%)
  between operations  17.6 us (9%)
  matrix products  4.48 us (2%)
    psum x1, blocking collectives, body(): lax.psum((local_total, picked_local), ('section', 'tensor'))  41 us
    pmax x1, blocking collectives, body(): row_top = lax.pmax(local_top, ('section', 'tensor'))  39.6 us
    reduce_scatter x1, waiting for transfers between devices, body(): lax.psum_scatter(lax.dot_general(out_weight, dlogits, (((0,), (1,)), ((),...  34.1 us
    reduce_scatter x1, waiting for transfers between devices, body(): lax.psum_scatter(width_part, 'section', scatter_dimension=1, tiled=True)  20.1 us
    all_gather x1, blocking collectives, body(): gathered = lax.all_gather(full_rows, 'section', axis=0, tiled=True)  16.3 us
    all_gather x1, blocking collectives, body(): full_rows = lax.all_gather(hidden, 'tensor', axis=1, tiled=True)  10.9 us
  transfers between devices with their start and end apart: 2, of which 2 were waited for; matrix products, arithmetic and copies ran while one was open for 1% of the time, Pallas kernels for 0%

commit v1 on v0

--- a/solution.py
+++ b/solution.py
@@ -23,7 +23,7 @@
     local_top = jnp.max(logits, axis=1)
     row_top = lax.pmax(local_top, ("section", "tensor"))
     local_total = jnp.sum(jnp.exp(logits - row_top[:, None]), axis=1)
-    row_total, picked = lax.psum((local_total, picked_local), ("section", "tensor"))
+    row_total, picked = lax.psum(lax.psum((local_total, picked_local), "tensor"), "section")
     log_total = row_top + jnp.log(row_total)
     kept = token_mask.astype(jnp.float32)
     ce_loss = jnp.sum(kept * (log_total - picked)) / token_count

time: 186 us -> 165 us (0.89)
  blocking collectives: 108 us -> 89.5 us
  waiting for transfers between devices: 54.2 us -> 51.5 us
    psum x1 -> x2, blocking collectives: 41 us -> 22.8 us  [the longest x1 12.7 us: body(): lax.psum((local_total, picked_local), 'tensor')]
    reduce_scatter x1, waiting for transfers between devices: 34.1 us -> 31.3 us  [body(): lax.psum_scatter(lax.dot_general(out_weight, dlogits, (((0,), (1,)), ((),...]
  transfers between devices with their start and end apart: 2 -> 2, of which waited for: 2 -> 2; matrix products, arithmetic and copies ran while one was open for 1% -> 2% of each run, Pallas kernels for 0% -> 0%
where the time goes in v1:
time: 165 us
  blocking collectives  89.5 us (54%)
  waiting for transfers between devices  51.5 us (31%)
  between operations  17.6 us (11%)
  matrix products  4.49 us (3%)
    pmax x1, blocking collectives, body(): row_top = lax.pmax(local_top, ('section', 'tensor'))  39.6 us
    reduce_scatter x1, waiting for transfers between devices, body(): lax.psum_scatter(lax.dot_general(out_weight, dlogits, (((0,), (1,)), ((),...  31.3 us
    reduce_scatter x1, waiting for transfers between devices, body(): lax.psum_scatter(width_part, 'section', scatter_dimension=1, tiled=True)  20.1 us
    all_gather x1, blocking collectives, body(): gathered = lax.all_gather(full_rows, 'section', axis=0, tiled=True)  16.3 us
    psum x1, blocking collectives, body(): lax.psum((local_total, picked_local), 'tensor')  12.7 us
    all_gather x1, blocking collectives, body(): full_rows = lax.all_gather(hidden, 'tensor', axis=1, tiled=True)  10.9 us
    psum x1, blocking collectives, body(): lax.psum(lax.psum((local_total, picked_local), 'tensor'), 'section')  10.1 us
  transfers between devices with their start and end apart: 2, of which 2 were waited for; matrix products, arithmetic and copies ran while one was open for 2% of the time, Pallas kernels for 0%

profile of v1, /device:TPU:0, one launch (start us, length us, event | category | flops | bytes accessed | tf_op | source)
XLA Modules:
  0.0 164.8 jit_solution(9147936822885530075)
XLA Ops:
  7.2 0.0 copy-start
  7.2 0.0 copy-start.2
  7.2 0.0 reduce-scatter.3.cloned.1.call-start
  7.2 0.8 convert_element_type.12
  8.0 10.9 %all_gather.6 = bf16[8,8192]{1,0:T(8,128)(2,1)S(1)} all-gather(bf16[8,1024]{1,0:T(8,128)(2,1)} %param.4), channel_id=1, replica_groups=mesh['section'=4,'tensor'=8] {'tensor'}, dimensions={1}, use_global_device_ids=true | all-gather | bytes 147456 | tf_op jit(solution)/shard_map/all_gather | solution.py:11
  18.9 16.3 %all_gather.7 = bf16[32,8192]{1,0:T(8,128)(2,1)S(1)} all-gather(bf16[8,8192]{1,0:T(8,128)(2,1)S(1)} %all_gather.6), channel_id=1, replica_groups=mesh['section'=4,'tensor'=8] {'section'}, dimensions={0}, use_global_device_ids=true | all-gather | bytes 655360 | tf_op jit(solution)/shard_map/all_gather | solution.py:12
  35.2 0.0 copy-done
  35.2 0.9 fusion.1
  36.1 39.6 %pmax.7 = f32[32]{0:T(128)S(1)} all-reduce(f32[32]{0:T(128)S(1)} %get-tuple-element.14), channel_id=1, replica_groups=mesh['section'=4,'tensor'=8] {'section','tensor'}, use_global_device_ids=true, to_apply=%region_1.2 | all-reduce | flops 32 | bytes 256 | tf_op jit(solution)/shard_map/pmax | solution.py:24
  75.7 0.0 copy-done.2
  75.7 0.2 select_reduce_fusion
  75.9 12.7 %all-reduce = (f32[32]{0:T(128)S(1)}, f32[32]{0:T(128)S(1)}) all-reduce(f32[32]{0:T(128)S(1)} %get-tuple-element.5, f32[32]{0:T(128)S(1)} %get-tuple-element.4), channel_id=1, replica_groups=mesh['section'=4,'tensor'=8] {'tensor'}, use_global_device_ids=true, to_apply=%region_3.4 | all-reduce | flops 64 | bytes 512 | tf_op jit(solution)/shard_map/psum | solution.py:26
  88.6 10.1 %all-reduce.1 = (f32[32]{0:T(128)S(1)}, f32[32]{0:T(128)S(1)}) all-reduce(f32[32]{0:T(128)S(1)} %get-tuple-element.8, f32[32]{0:T(128)S(1)} %get-tuple-element.9), channel_id=1, replica_groups=mesh['section'=4,'tensor'=8] {'section'}, use_global_device_ids=true, to_apply=%region_4.5 | all-reduce | flops 64 | bytes 512 | tf_op jit(solution)/shard_map/psum | solution.py:26
  98.7 0.0 copy-start.1
  98.7 1.4 convolution_bitcast_fusion
  100.1 0.0 reduce-scatter.3.cloned.1.call-update
  100.1 0.0 reduce-scatter.5.cloned.1.call-start
  100.2 0.0 copy-done.1
  100.2 0.6 fusion
  102.1 31.3 %reduce-scatter.3.cloned.1.call-done = f32[1024,32]{0,1:T(8,128)} async-done(((f32[8192,32]{0,1:T(8,128)}), f32[1024,32]{0,1:T(8,128)}) %reduce-scatter.3.cloned.1.call-update) | async-done | bytes 131088 | tf_op jit(solution)/shard_map/reduce_scatter | solution.py:39
  133.4 0.0 reduce-scatter.5.cloned.1.call-update
  133.5 2.1 %convolution_convert_fusion = bf16[128,8192]{1,0:T(8,128)(2,1)} fusion(bf16[32,8192]{1,0:T(8,128)(2,1)S(1)} %all_gather.7, f32[32,128]{1,0:T(8,128)S(1)} %get-tuple-element.15, f32[32]{0:T(128)S(1)} %get-tuple-element.13, f32[32]{0:T(128)S(1)} %get-tuple-element.12, f32[32]{0:T(128)S(1)} %convert_element_type.12, s32[32]{0:T(128)S(1)} %broadcast_subtract_fusion), kind=kOutput, calls=%fused_computation | convolution fusion | flops 68186112 | bytes 2638336 | tf_op jit(solution)/shard_map/dot_general | solution.py:36
  135.6 20.1 %reduce-scatter.5.cloned.1.call-done = f32[1024,8]{0,1:T(8,128)} async-done(((f32[1024,32]{0,1:T(8,128)}), f32[1024,8]{0,1:T(8,128)}) %reduce-scatter.5.cloned.1.call-update) | async-done | bytes 32784 | tf_op jit(solution)/shard_map/reduce_scatter | solution.py:47
  (2 shorter events, 0.0 us)
Async XLA Ops:
  7.2 28.1 %copy-start = (bf16[128,8192]{1,0:T(8,128)(2,1)S(1)}, bf16[128,8192]{1,0:T(8,128)(2,1)}, u32[]{:S(2)}) copy-start(bf16[128,8192]{1,0:T(8,128)(2,1)} %param.5) | copy-start | bytes 6291460
  7.2 68.5 %copy-start.2 = (s32[32]{0:T(128)S(1)}, s32[32]{0:T(128)}, u32[]{:S(2)}) copy-start(s32[32]{0:T(128)} %param.6) | copy-start | bytes 388
  7.2 126.3 %reduce-scatter.3.cloned.1.call-start = ((), (), s32[]{:S(2)}) async-start(), calls=%async_computation.2 | async-start | bytes 1179648 | tf_op jit(solution)/shard_map/reduce_scatter | solution.py:39
  98.7 1.5 copy-start.1
  100.1 55.6 %reduce-scatter.5.cloned.1.call-start = ((), (), s32[]{:S(2)}) async-start(), calls=%async_computation.3 | async-start | bytes 163840 | tf_op jit(solution)/shard_map/reduce_scatter | solution.py:47
Sparse Core Ops, SparseCore 0:
  100.3 33.1 reduce-scatter.2
  136.3 19.4 reduce-scatter.4
